TPU v7x, 32 devices: a whole 2x2x4 slice. The times are simulated.
32 devices in a mesh: dp: 8 (over z, y), mp: 4 (over x, core).
Axes of the slice: x: 2, y: 2, z: 4, core: 2. Of those that a mesh axis runs over, the one named last changes fastest.
Arguments:
- patches: bfloat16 [24, 1024, 1280], P('dp', 'mp'), may hold values from -6 to 6
- kept_mask: int32 [24, 1024], P('dp', 'mp'), may hold values from 0 to 1, as said below
- destination: int32 [24, 1024], P('dp', 'mp'), may hold values from 0 to 7, as said below
- coefficients: bfloat16 [9, 1280, 2560], P(None, None, 'mp'), may hold values from -0.15625 to 0.15625
- cotangent: bfloat16 [6144, 2560], P('dp', 'mp'), may hold values from -3 to 3
Outputs:
- grad_patches: bfloat16 [24, 1024, 1280], P('dp', 'mp')
- grad_coefficients: float32 [9, 1280, 2560], P(None, 'dp', 'mp')
Inputs may be any that keep to these rules, and one draw needn't show every extreme that they name: `kept_mask`: every image keeps the same number of patches in each of its 4 blocks, from 32 to 96; all images together keep exactly 6144 patches. For a kept patch, its balanced shard; entries of patches that are not kept are not used. Among the kept patches of one block of the 3 images of one index of dp, at most 36 have the same destination, and some index of dp has exactly 36 for every destination in every block. Every destination receives exactly 192 kept patches of each block.
All inputs are finite; a program needn't handle non-finite values.
Results may differ from a plain program's by a relative error of at most 0.0074.
Values may be sent and summed in bfloat16 or wider, within the bound.
No kernel may reach another device: no remote copies, remote signals or barrier semaphores. Data moves between devices by JAX's collectives and lax.ppermute only.
A program may use at most 192 MiB of HBM per device.

v0:
```python
import jax
import jax.numpy as jnp
from jax import lax
from jax.sharding import PartitionSpec as P

NBASIS = 8
KEEP_IMG = 256


STEP_WIDTH = 0.8
FIRST_KNOT = -4.4
EPSILON = 1e-05


def inner_piece(value):
    return (((-3.0 * value + 12.0) * value - 12.0) * value + 4.0) / 6.0


def inner_slope(value):
    return ((-3.0 * value + 8.0) * value - 4.0) / 2.0


def cardinal(scaled):
    mirror = 4.0 - scaled
    result = jnp.where(
        scaled < 1.0,
        scaled * scaled * scaled / 6.0,
        jnp.where(
            scaled < 2.0,
            inner_piece(scaled),
            jnp.where(scaled < 3.0, inner_piece(mirror), mirror * mirror * mirror / 6.0),
        ),
    )
    return jnp.where((scaled >= 0.0) & (scaled < 4.0), result, 0.0)


def cardinal_slope(scaled):
    mirror = 4.0 - scaled
    result = jnp.where(
        scaled < 1.0,
        scaled * scaled / 2.0,
        jnp.where(
            scaled < 2.0,
            inner_slope(scaled),
            jnp.where(scaled < 3.0, -inner_slope(mirror), -mirror * mirror / 2.0),
        ),
    )
    return jnp.where((scaled >= 0.0) & (scaled < 4.0), result, 0.0)


def knot_offsets(values):
    knots = (FIRST_KNOT + STEP_WIDTH * jnp.arange(NBASIS).astype(jnp.float32)).reshape(1, NBASIS, 1)
    return (values[:, None, :] - knots) / STEP_WIDTH


def expand(values):
    sigmoid = jax.nn.sigmoid(values)
    return jnp.concatenate([(values * sigmoid)[:, None, :], cardinal(knot_offsets(values))], axis=1)


def expand_slope(values):
    sigmoid = jax.nn.sigmoid(values)
    base_slope = sigmoid * (1.0 + values * (1.0 - sigmoid))
    return jnp.concatenate(
        [base_slope[:, None, :], cardinal_slope(knot_offsets(values)) / STEP_WIDTH], axis=1
    )


def normalize(rows):
    wide = rows.astype(jnp.float32)
    centre = jnp.mean(wide, axis=1, keepdims=True)
    spread = jnp.mean((wide - centre) * (wide - centre), axis=1, keepdims=True)
    inv_scale = lax.rsqrt(spread + EPSILON)
    return ((wide - centre) * inv_scale, inv_scale)


def on_device(patches, kept_mask, destination, coefficients, cotangent):
    dp_count = lax.axis_size("dp")
    mp_count = lax.axis_size("mp")
    img_dev, block_len, features = patches.shape
    channels = coefficients.shape[0]
    hidden = coefficients.shape[2]
    capacity = img_dev * (KEEP_IMG // mp_count + KEEP_IMG // (2 * mp_count)) // dp_count
    own_rows = img_dev * (KEEP_IMG // mp_count)
    slot_total = dp_count * capacity
    flat_rows = patches.reshape(img_dev * block_len, features)
    is_kept = kept_mask.reshape(-1) == 1
    target = destination.reshape(-1)
    shards = jnp.arange(dp_count, dtype=jnp.int32)
    onehot = ((target[:, None] == shards[None, :]) & is_kept[:, None]).astype(jnp.int32)
    earlier = jnp.cumsum(onehot, axis=0) - onehot
    slot_rank = jnp.sum(earlier * onehot, axis=1)
    counts = jnp.sum(onehot, axis=0)
    position = jnp.where(is_kept, target * capacity + slot_rank, slot_total)
    outgoing = (
        jnp.zeros((slot_total, features), jnp.bfloat16).at[position].set(flat_rows, mode="drop")
    )
    arrived, arrived_counts = (
        lax.all_to_all(outgoing, "dp", split_axis=0, concat_axis=0, tiled=True),
        lax.all_to_all(counts.reshape(dp_count, 1), "dp", split_axis=0, concat_axis=0, tiled=True),
    )
    from_each = arrived_counts.reshape(dp_count)
    offsets = jnp.cumsum(from_each).astype(jnp.int32) - from_each
    slot_index = jnp.arange(capacity, dtype=jnp.int32)
    in_use = (slot_index[None, :] < from_each[:, None]).reshape(-1)
    compact_at = jnp.where(
        in_use, (offsets[:, None] + slot_index[None, :]).reshape(-1), own_rows
    ).astype(jnp.int32)
    local_rows = (
        jnp.zeros((own_rows, features), jnp.bfloat16).at[compact_at].set(arrived, mode="drop")
    )
    centred, inv_scale = normalize(local_rows)
    normed = centred.astype(jnp.bfloat16)
    normed_all = lax.all_gather(normed, "mp", axis=0, tiled=True)
    normed_wide = normed_all.astype(jnp.float32)
    coef_table = coefficients.reshape(channels * features, hidden)
    expanded = expand(normed_wide).astype(jnp.bfloat16)
    coef_share = lax.psum_scatter(
        jnp.einsum("tkf,tj->fkj", expanded, cotangent, preferred_element_type=jnp.float32),
        "dp",
        scatter_dimension=0,
        tiled=True,
    )
    grad_coefficients = coef_share.transpose(1, 0, 2)
    piece_count = own_rows * lax.axis_size("mp") // own_rows

    def one_piece(piece_index):
        start = piece_index * own_rows
        cot_rows = lax.dynamic_slice_in_dim(cotangent, start, own_rows, 0)
        value_rows = lax.dynamic_slice_in_dim(normed_wide, start, own_rows, 0)
        hidden_grad = lax.dot_general(
            cot_rows, coef_table, (((1,), (1,)), ((), ())), preferred_element_type=jnp.float32
        ).reshape(own_rows, channels, features)
        return jnp.sum(hidden_grad * expand_slope(value_rows), axis=1)

    pieces = lax.map(one_piece, jnp.arange(piece_count, dtype=jnp.int32))
    normed_grad = lax.psum_scatter(
        pieces.reshape(own_rows * lax.axis_size("mp"), features),
        "mp",
        scatter_dimension=0,
        tiled=True,
    )
    first_mean = jnp.mean(normed_grad, axis=1, keepdims=True)
    second_mean = jnp.mean(normed_grad * centred, axis=1, keepdims=True)
    row_grad = (inv_scale * (normed_grad - first_mean - centred * second_mean)).astype(jnp.bfloat16)
    source_rows = jnp.minimum(compact_at, own_rows - 1)
    back_slots = jnp.where(in_use[:, None], row_grad[source_rows], jnp.zeros((), jnp.bfloat16))
    returned = lax.all_to_all(back_slots, "dp", split_axis=0, concat_axis=0, tiled=True)
    clamped = jnp.minimum(position, slot_total - 1)
    owner_rows = jnp.where(is_kept[:, None], returned[clamped], jnp.zeros((), jnp.bfloat16))
    grad_patches = owner_rows.reshape(img_dev, block_len, features)
    return (grad_patches, grad_coefficients)


def solution(mesh):
    in_specs = (
        P("dp", "mp", None),
        P("dp", "mp"),
        P("dp", "mp"),
        P(None, None, "mp"),
        P("dp", "mp"),
    )
    out_specs = (P("dp", "mp", None), P(None, "dp", "mp"))
    return jax.shard_map(
        on_device, mesh=mesh, in_specs=in_specs, out_specs=out_specs, check_vma=False
    )
```

profile of v0, /device:TPU:0, one launch (start us, length us, event | category | flops | bytes accessed | tf_op | source)
XLA Modules:
  0.0 766.5 jit_solution(5682061262175432211)
XLA Ops:
  12.3 7.3 all-to-all-start
  21.6 6.8 scatter_custom_fusion
  29.4 6.0 all-to-all-start.1
  37.0 18.8 %all-to-all-done.1 = bf16[8,36,1280]{2,1,0:T(8,128)(2,1)S(1)} async-done(((bf16[8,36,1280]{2,1,0:T(8,128)(2,1)}), bf16[8,36,1280]{2,1,0:T(8,128)(2,1)S(1)}, u32[]{:S(2)}, u32[]{:S(2)}) %all-to-all-start.1) | async-done | bytes 737312 | tf_op jit(solution)/shard_map/all_to_all | solution.py:99
  60.6 20.6 %all-gather.2.cloned.1.call-done = bf16[768,1280]{1,0:T(8,128)(2,1)} async-done(((bf16[192,1280]{1,0:T(8,128)(2,1)}), bf16[768,1280]{1,0:T(8,128)(2,1)}) %all-gather.2.cloned.1.call-update) | async-done | bytes 1966096 | tf_op jit(solution)/shard_map/all_gather | solution.py:114
  86.4 119.0 %while.13 = (s32[]{:T(128)}, f32[4,192,1280]{2,1,0:T(8,128)}, s32[4]{0:T(128)S(1)}, bf16[768,640]{1,0:T(8,128)(2,1)}, bf16[11520,640]{1,0:T(8,128)(2,1)}, /*inde...) while((s32[]{:T(128)}, f32[4,192,1280]{2,1,0:T(8,128)}, s32[4]{0:T(128)S(1)}, ...), condition=%wide.region_11.12_spmd, body=%wide.region_9.11_spmd.sunk | while | flops 2898247680 | bytes 58245364 | solution.py:136
  90.8 10.1 %fusion.96 = f32[192,8,1280]{0,2,1:T(8,128)S(1)} fusion(f32[8]{0:T(128)S(1)} %multiply_add_fusion.3, f32[192,1280]{0,1:T(8,128)S(1)} %get-tuple-element.170), kind=kLoop, calls=%fused_computation.27.clone.1 | loop fusion | flops 58982400 | bytes 8847392 | tf_op jit(solution)/shard_map/while/body/eval_jaxpr/div | solution.py:65
  100.9 8.3 %fusion.95 = f32[192,11520]{0,1:T(8,128)S(1)} fusion(bf16[11520,640]{1,0:T(8,128)(2,1)} %get-tuple-element.196, bf16[768,640]{1,0:T(8,128)(2,1)} %get-tuple-element.195, s32[]{:T(128)S(6)} %select_n.221), kind=kOutput, calls=%fused_computation.35.clone.1 | convolution fusion | flops 2831155200 | bytes 23838724 | tf_op jit(solution)/shard_map/while/body/eval_jaxpr/dot_general | solution.py:131
  109.2 4.3 fusion.97
  117.5 3.1 multiply_bitcast_fusion.3
  120.6 10.1 %fusion.96 = f32[192,8,1280]{0,2,1:T(8,128)S(1)} fusion(f32[8]{0:T(128)S(1)} %multiply_add_fusion.3, f32[192,1280]{0,1:T(8,128)S(1)} %get-tuple-element.170), kind=kLoop, calls=%fused_computation.27.clone.1 | loop fusion | flops 58982400 | bytes 8847392 | tf_op jit(solution)/shard_map/while/body/eval_jaxpr/div | solution.py:65
  130.6 8.4 %fusion.95 = f32[192,11520]{0,1:T(8,128)S(1)} fusion(bf16[11520,640]{1,0:T(8,128)(2,1)} %get-tuple-element.196, bf16[768,640]{1,0:T(8,128)(2,1)} %get-tuple-element.195, s32[]{:T(128)S(6)} %select_n.221), kind=kOutput, calls=%fused_computation.35.clone.1 | convolution fusion | flops 2831155200 | bytes 23838724 | tf_op jit(solution)/shard_map/while/body/eval_jaxpr/dot_general | solution.py:131
  139.0 4.3 fusion.97
  150.4 10.1 %fusion.96 = f32[192,8,1280]{0,2,1:T(8,128)S(1)} fusion(f32[8]{0:T(128)S(1)} %multiply_add_fusion.3, f32[192,1280]{0,1:T(8,128)S(1)} %get-tuple-element.170), kind=kLoop, calls=%fused_computation.27.clone.1 | loop fusion | flops 58982400 | bytes 8847392 | tf_op jit(solution)/shard_map/while/body/eval_jaxpr/div | solution.py:65
  160.5 8.3 %fusion.95 = f32[192,11520]{0,1:T(8,128)S(1)} fusion(bf16[11520,640]{1,0:T(8,128)(2,1)} %get-tuple-element.196, bf16[768,640]{1,0:T(8,128)(2,1)} %get-tuple-element.195, s32[]{:T(128)S(6)} %select_n.221), kind=kOutput, calls=%fused_computation.35.clone.1 | convolution fusion | flops 2831155200 | bytes 23838724 | tf_op jit(solution)/shard_map/while/body/eval_jaxpr/dot_general | solution.py:131
  168.8 4.3 fusion.97
  180.0 10.1 %fusion.96 = f32[192,8,1280]{0,2,1:T(8,128)S(1)} fusion(f32[8]{0:T(128)S(1)} %multiply_add_fusion.3, f32[192,1280]{0,1:T(8,128)S(1)} %get-tuple-element.170), kind=kLoop, calls=%fused_computation.27.clone.1 | loop fusion | flops 58982400 | bytes 8847392 | tf_op jit(solution)/shard_map/while/body/eval_jaxpr/div | solution.py:65
  190.1 8.3 %fusion.95 = f32[192,11520]{0,1:T(8,128)S(1)} fusion(bf16[11520,640]{1,0:T(8,128)(2,1)} %get-tuple-element.196, bf16[768,640]{1,0:T(8,128)(2,1)} %get-tuple-element.195, s32[]{:T(128)S(6)} %select_n.221), kind=kOutput, calls=%fused_computation.35.clone.1 | convolution fusion | flops 2831155200 | bytes 23838724 | tf_op jit(solution)/shard_map/while/body/eval_jaxpr/dot_general | solution.py:131
  198.4 4.3 fusion.97
  205.8 40.8 %fusion.54 = bf16[768,8,1280]{0,2,1:T(8,128)(2,1)} fusion(f32[8]{0:T(128)S(1)} %multiply_add_fusion.1, f32[768,1280]{0,1:T(8,128)} %get-tuple-element.205), kind=kLoop, calls=%fused_computation.70 | loop fusion | flops 267386880 | bytes 19660832 | tf_op jit(solution)/shard_map/convert.1
  248.9 22.9 %convolution_bitcast_fusion = f32[1280,9,640]{2,0,1:T(8,128)} fusion(bf16[768,8,1280]{0,2,1:T(8,128)(2,1)} %fusion.54, bf16[768,1,1280]{0,2,1:T(8,128)(2,1)} %fusion.59, bf16[768,640]{1,0:T(8,128)(2,1)S(1)} %copy-done.4), kind=kOutput, calls=%fused_computation.72 | convolution fusion | flops 11333468160 | bytes 48168960 | tf_op jit(solution)/shard_map/tkf,tj->fkj/dot_general | solution.py:119
  279.5 5.7 all-to-all-start.2
  285.2 44.3 %all-to-all-done.2 = bf16[8,36,1280]{2,1,0:T(8,128)(2,1)S(1)} async-done(((bf16[8,36,1280]{2,1,0:T(8,128)(2,1)}), bf16[8,36,1280]{2,1,0:T(8,128)(2,1)S(1)}, u32[]{:S(2)}, u32[]{:S(2)}) %all-to-all-start.2) | async-done | bytes 737312 | tf_op jit(solution)/shard_map/all_to_all | solution.py:148
  334.0 426.0 %reduce-scatter.5.cloned.1.call-done = f32[160,9,640]{2,0,1:T(8,128)} async-done(((f32[1280,9,640]{2,0,1:T(8,128)}), f32[160,9,640]{2,0,1:T(8,128)}) %reduce-scatter.5.cloned.1.call-update) | async-done | bytes 3686416 | tf_op jit(solution)/shard_map/reduce_scatter | solution.py:118
  (107 shorter events, 56.7 us)
Async XLA Ops:
  7.9 1.4 copy-start.7
  12.3 17.2 %all-to-all-start = ((s32[8,1,1]{2,1,0:T(1,128)}), s32[8,1,1]{2,1,0:T(1,128)S(1)}, u32[]{:S(2)}, u32[]{:S(2)}) async-start(s32[8,1,1]{2,1,0:T(1,128)} %copy.29), calls=%async_computation | async-start | bytes 8192 | tf_op jit(solution)/shard_map/all_to_all | solution.py:100
  29.4 26.4 %all-to-all-start.1 = ((bf16[8,36,1280]{2,1,0:T(8,128)(2,1)}), bf16[8,36,1280]{2,1,0:T(8,128)(2,1)S(1)}, u32[]{:S(2)}, u32[]{:S(2)}) async-start(bf16[8,36,1280]{2,1,0:T(8,128)(2,1)} %all_to_all.22), calls=%async_computation.1 | async-start | bytes 1638400 | tf_op jit(solution)/shard_map/all_to_all | solution.py:99
  35.4 45.7 %all-gather.2.cloned.1.call-start = ((), (), s32[]{:S(2)}) async-start(), calls=%async_computation.5 | async-start | bytes 2457600 | tf_op jit(solution)/shard_map/all_gather | solution.py:114
  35.7 0.5 copy-start.13
  58.0 2.6 copy-start.2
  58.1 0.6 copy-start.5
  58.7 0.6 copy-start.10
  60.3 212.2 %reduce-scatter.7.cloned.1.call-start = ((), (), s32[]{:S(2)}) async-start(), calls=%async_computation.7 | async-start | bytes 4915200 | tf_op jit(solution)/shard_map/reduce_scatter | solution.py:137
  83.9 2.6 copy-start
  205.5 41.1 %copy-start.1 = (bf16[768,1280]{0,1:T(8,128)(2,1)S(1)}, bf16[768,1280]{0,1:T(8,128)(2,1)}, u32[]{:S(2)}) copy-start(bf16[768,1280]{0,1:T(8,128)(2,1)} %copy-done) | copy-start | bytes 5898244
  205.5 43.4 %copy-start.4 = (bf16[768,640]{1,0:T(8,128)(2,1)S(1)}, bf16[768,640]{1,0:T(8,128)(2,1)}, u32[]{:S(2)}) copy-start(bf16[768,640]{1,0:T(8,128)(2,1)} %get-tuple-element.216) | copy-start | bytes 2949124
  205.5 554.5 %reduce-scatter.5.cloned.1.call-start = ((), (), s32[]{:S(2)}) async-start(), calls=%async_computation.6 | async-start | bytes 33177600 | tf_op jit(solution)/shard_map/reduce_scatter | solution.py:118
  271.8 0.7 copy-start.12
  271.8 0.7 copy-start.14
  271.8 1.0 copy-start.3
  271.8 1.0 copy-start.6
  271.8 1.0 copy-start.11
  271.8 13.3 %copy-start.9 = (s32[768]{0:T(1024)S(1)}, s32[768]{0:T(1024)}, u32[]{:S(2)}) copy-start(s32[768]{0:T(1024)} %get-tuple-element.111) | copy-start | bytes 9220
  279.5 53.1 %copy-start.8 = (pred[3,256]{1,0:T(4,128)(4,1)S(1)}, pred[3,256]{1,0:T(4,128)(4,1)}, u32[]{:S(2)}) copy-start(pred[3,256]{1,0:T(4,128)(4,1)} %copy-done.7) | copy-start | bytes 2308
  279.5 50.0 %all-to-all-start.2 = ((bf16[8,36,1280]{2,1,0:T(8,128)(2,1)}), bf16[8,36,1280]{2,1,0:T(8,128)(2,1)S(1)}, u32[]{:S(2)}, u32[]{:S(2)}) async-start(bf16[8,36,1280]{2,1,0:T(8,128)(2,1)} %broadcast_select_fusion.1), calls=%async_computation.2 | async-start | bytes 1638400 | tf_op jit(solution)/shard_map/all_to_all | solution.py:148
Sparse Core Ops, SparseCore 0:
  60.4 20.6 all-gather.1
  205.6 42.9 reduce-scatter.6
  272.0 487.9 reduce-scatter.4
where the time goes:
time: 768 us; the launch traced here: 767 us
  waiting for transfers between devices  510 us (66%)
  other arithmetic  128 us (17%)
  matrix products  56.2 us (7%)
  local copies, waits for them, and re-layouts  36.1 us (5%)
  starting transfers between devices  19.5 us (3%)
  between operations  14 us (2%)
    reduce_scatter x1, waiting for transfers between devices, on_device(): lax.psum_scatter(jnp.einsum('tkf,tj->fkj', expanded, cotangent, preferred...  426 us
    all_to_all x1, waiting for transfers between devices, on_device(): lax.all_to_all(back_slots, 'dp', split_axis=0, concat_axis=0, tiled=True)  44.3 us
    another operation x4, other arithmetic  42.8 us
    div x4, other arithmetic, expand_slope(): cardinal_slope(knot_offsets(values)) / STEP_WIDTH  40.3 us
    dot_general x4, matrix products, one_piece(): lax.dot_general(cot_rows, coef_table, (((1,), (1,)), ((), ())), preferred...  33.4 us
    dot_general x1, matrix products, on_device(): jnp.einsum('tkf,tj->fkj', expanded, cotangent, preferred_element_type=jnp...  22.9 us
    all_gather x1, waiting for transfers between devices, on_device(): normed_all = lax.all_gather(normed, 'mp', axis=0, tiled=True)  20.6 us
    all_to_all x1, waiting for transfers between devices, on_device(): lax.all_to_all(outgoing, 'dp', split_axis=0, concat_axis=0, tiled=True)  18.8 us
  transfers between devices with their start and end apart: 6, of which 4 were waited for; matrix products, arithmetic and copies ran while one was open for 11% of the time, Pallas kernels for 0%

commit v1 on v0

v1 whole, which is shorter than its diff:
```python
import functools

import jax
import jax.numpy as jnp
import numpy as np
from jax import lax
from jax.experimental import pallas as pl
from jax.experimental.pallas import tpu as pltpu
from jax.sharding import PartitionSpec as P

KEEP_IMG = 256
FIRST_KNOT = -4.4
INV_STEP = 1.25
EPSILON = 1e-05
BF = jnp.bfloat16
F32 = jnp.float32
NBASIS = 8
PARAMS = pltpu.CompilerParams(vmem_limit_bytes=58 * 2**20)


def cost(flops, moved):
    return pl.CostEstimate(flops=int(flops), transcendentals=0, bytes_accessed=int(moved))


def cell_of(wide):
    scaled = (wide - FIRST_KNOT) * INV_STEP
    cell = jnp.floor(scaled)
    frac = scaled - cell
    legal = (cell >= 0.0) & (cell <= 10.0)
    return jnp.where(legal, cell, 11.0), frac


def bits_of(cell):
    low = cell
    bits = []
    for weight in (8.0, 4.0, 2.0):
        has = low >= weight
        low = jnp.where(has, low - weight, low)
        bits.append(has)
    bits.append(low >= 1.0)
    return bits


def sigmoid(wide):
    return 1.0 / (1.0 + jnp.exp(-wide))


def spread_basis(wide):
    cell, frac = cell_of(wide)
    bit8, bit4, bit2, bit1 = bits_of(cell.astype(BF))
    square = frac * frac
    cube = square * frac
    mirror = 1.0 - frac
    p0 = cube * (1.0 / 6.0)
    p1 = (1.0 + 3.0 * (frac + square - cube)) * (1.0 / 6.0)
    p2 = (4.0 - 6.0 * square + 3.0 * cube) * (1.0 / 6.0)
    p3 = mirror * mirror * mirror * (1.0 / 6.0)
    lane = [p.astype(BF) for p in (p3, p2, p1, p0)]
    zero = jnp.zeros_like(lane[0])

    def at(items, index):
        return items[index] if 0 <= index < len(items) else zero

    for bit, shift, size in ((bit1, 1, 5), (bit2, 2, 7), (bit4, 4, 11)):
        lane = [jnp.where(bit, at(lane, i - shift), at(lane, i)) for i in range(size)]
    tops = [jnp.where(bit8, at(lane, i - 8), at(lane, i)) for i in range(3, 11)]
    return [(wide * sigmoid(wide)).astype(BF)] + tops


def slope_sum(wide, base_grad, grads):
    cell, frac = cell_of(wide)
    bit8, bit4, bit2, bit1 = bits_of(cell.astype(BF))
    zero = jnp.zeros_like(grads[0])
    row = [zero] * 3 + grads + [zero] * 4
    row = [jnp.where(bit8, row[i + 8], row[i]) if i < 7 else row[i] for i in range(11)]
    row = [jnp.where(bit4, row[i + 4], row[i]) for i in range(7)]
    row = [jnp.where(bit2, row[i + 2], row[i]) for i in range(5)]
    row = [jnp.where(bit1, row[i + 1], row[i]) for i in range(4)]
    half = 0.5 * INV_STEP
    square3 = 3.0 * frac * frac
    mirror = 1.0 - frac
    q0 = frac * frac
    q1 = 1.0 + 2.0 * frac - square3
    q2 = square3 - 4.0 * frac
    q3 = -(mirror * mirror)
    spline = q0 * row[3].astype(F32) + q1 * row[2].astype(F32)
    spline = spline + q2 * row[1].astype(F32) + q3 * row[0].astype(F32)
    sig = sigmoid(wide)
    return spline * half + base_grad.astype(F32) * (sig * (1.0 + wide * (1.0 - sig)))


def send_kernel(n_dest, slots, capacity, kept_ref, dest_ref, rows_ref, out_ref, at_ref):
    images = kept_ref.shape[0]
    total = n_dest * slots
    kept = jnp.concatenate([kept_ref[i : i + 1, :] for i in range(images)], axis=1)
    dest = jnp.concatenate([dest_ref[i : i + 1, :] for i in range(images)], axis=1)
    count = kept.shape[1]
    padded = max(16, n_dest)
    shard = lax.broadcasted_iota(jnp.int32, (padded, count), 0)
    onehot = jnp.where((shard == dest) & (kept == 1), 1.0, 0.0).astype(F32)
    before = (
        lax.broadcasted_iota(jnp.int32, (count, count), 0)
        < lax.broadcasted_iota(jnp.int32, (count, count), 1)
    ).astype(F32).astype(BF)
    earlier = jnp.dot(onehot.astype(BF), before, preferred_element_type=F32)
    rank = jnp.sum((earlier + shard.astype(F32) * slots) * onehot, axis=0, keepdims=True)
    place = jnp.where(kept == 1, rank, -1.0).astype(jnp.int32)
    at_ref[...] = place
    pick = (lax.broadcasted_iota(jnp.int32, (total, count), 0) == place).astype(F32).astype(BF)
    moved = jnp.dot(pick, rows_ref[...], preferred_element_type=F32)
    counts = jnp.sum(onehot, axis=1, keepdims=True)
    counts = jnp.broadcast_to(counts, (padded, rows_ref.shape[1])).astype(BF)
    marks = (
        lax.broadcasted_iota(jnp.int32, (total, padded), 0)
        == lax.broadcasted_iota(jnp.int32, (total, padded), 1) * slots + capacity
    ).astype(F32).astype(BF)
    out_ref[...] = (moved + jnp.dot(marks, counts, preferred_element_type=F32)).astype(BF)


def arrive_kernel(
    n_dest, slots, capacity, own, in_ref, norm_ref, feat_ref, wide_ref, inv_ref, pick_ref, hold
):
    width = -(-own // 128) * 128
    row = lax.broadcasted_iota(jnp.int32, (slots, width), 0).astype(F32)
    lane = lax.broadcasted_iota(jnp.int32, (slots, width), 1).astype(F32)
    base = (capacity // 8) * 8
    start = jnp.zeros((1, width), F32)
    for source in range(n_dest):
        tile = in_ref[source, base : base + 8, 0:width].astype(F32)
        held = tile[capacity - base : capacity - base + 1, :]
        hit = (row < held) & (lane == start + row)
        hold[source * slots : (source + 1) * slots, :] = jnp.where(hit, 1.0, 0.0)
        start = start + held
    pick = hold[...].astype(BF)
    pick_ref[...] = pick
    rows = in_ref[...].reshape(n_dest * slots, in_ref.shape[2])
    local = lax.dot_general(pick, rows, (((0,), (0,)), ((), ())), preferred_element_type=F32)
    centre = jnp.mean(local, axis=1, keepdims=True)
    centred = local - centre
    spread = jnp.mean(centred * centred, axis=1, keepdims=True)
    inv = lax.rsqrt(spread + EPSILON)
    centred = centred * inv
    wide_ref[...] = centred[0:own]
    inv_ref[...] = jnp.broadcast_to(inv, (width, 128))[0:own]
    normed = centred[0:own].astype(BF)
    norm_ref[...] = normed
    turned = jnp.transpose(centred)
    step = turned.shape[0] // n_dest
    for dest in range(n_dest):
        upper = turned[dest * step : dest * step + step // 2, 0:own]
        lower = turned[dest * step + step // 2 : (dest + 1) * step, 0:own]
        feat_ref[dest] = jnp.concatenate([upper, lower], axis=1).astype(BF)


def hidden_kernel(cot_ref, coef_ref, out_ref):
    features = coef_ref.shape[1]
    for first in range(0, features, 256):
        out_ref[0, :, first : first + 256] = lax.dot_general(
            cot_ref[...],
            coef_ref[0, first : first + 256, :],
            (((1,), (1,)), ((), ())),
            preferred_element_type=F32,
        ).astype(BF)


def slope_kernel(groups, meta_ref, *refs):
    grads, value_ref, out_ref = refs[:groups], refs[groups], refs[groups + 1]
    rows, width = value_ref.shape

    def step(index, carry):
        span = pl.ds(pl.multiple_of(index * 16, 16), 16)
        wide = value_ref[span, :].astype(F32)
        parts = []
        for ref in grads:
            parts += [ref[c, span, :] for c in range(ref.shape[0])]
        out_ref[span, :] = slope_sum(wide, parts[0], parts[1:]).astype(out_ref.dtype)
        return carry

    lax.fori_loop(0, rows // 16, step, 0)


def merge_kernel(meta_ref, own_ref, core_ref, far_ref, diag_ref, out_ref):
    here = meta_ref[0]
    own, core, far, diag = own_ref[0], core_ref[0], far_ref[0], diag_ref[0]
    odd, high = lax.rem(here, 2) == 1, here >= 2

    def order(flag, first, second):
        return jnp.where(flag, second, first), jnp.where(flag, first, second)

    near = order(odd, own.astype(F32), core.astype(F32))
    away = order(odd, far.astype(F32), diag.astype(F32))
    low0, high0 = order(high, near[0], away[0])
    low1, high1 = order(high, near[1], away[1])
    pieces = [low0, low1, high0, high1]
    half = own.shape[0]
    count = own.shape[1] // 2
    upper = jnp.concatenate([piece[:, 0:count] for piece in pieces], axis=1)
    lower = jnp.concatenate([piece[:, count:] for piece in pieces], axis=1)
    out_ref[0, 0:half, :] = upper.astype(BF)
    out_ref[0, half:, :] = lower.astype(BF)


def table_kernel(spans, has_start, meta_ref, *refs):
    count = len(spans)
    values, cots = refs[:count], refs[count : 2 * count]
    start_ref = refs[2 * count] if has_start else None
    out_ref, hold = refs[-2], refs[-1]
    features = values[0].shape[1]
    hidden = cots[0].shape[1]
    for index, (low, high) in enumerate(spans):
        value_ref = values[index]

        def fill(span, value_ref=value_ref, low=low, high=high):
            for first in range(low, high, 128):
                wide = value_ref[0, span, first : first + 128].astype(F32)
                for channel, item in enumerate(spread_basis(wide)):
                    hold[channel, span, first - low : first - low + 128] = item

        def step(block, carry, fill=fill):
            fill(pl.ds(pl.multiple_of(block * 16, 16), 16))
            return carry

        if features % 16 == 0:
            lax.fori_loop(0, features // 16, step, 0)
        else:
            fill(slice(0, features))
        for channel in range(out_ref.shape[0]):
            total = jnp.dot(
                hold[channel, :, 0 : high - low], cots[index][...], preferred_element_type=F32
            )
            if index == 0 and has_start:
                total = total + start_ref[channel]
            if index > 0:
                total = total + out_ref[channel]
            out_ref[channel] = total


def reduce_kernel(own_ref, core_ref, far_ref, wide_ref, inv_ref, pick_ref, out_ref):
    grad = own_ref[...] + core_ref[...].astype(F32) + far_ref[...].astype(F32)
    wide = wide_ref[...]
    first = jnp.mean(grad, axis=1, keepdims=True)
    second = jnp.mean(grad * wide, axis=1, keepdims=True)
    row_grad = (inv_ref[:, 0:1] * (grad - first - wide * second)).astype(BF)
    own = row_grad.shape[0]
    back = jnp.dot(pick_ref[:, 0:own], row_grad, preferred_element_type=F32)
    out_ref[...] = back.astype(BF).reshape(out_ref.shape)


def place_kernel(at_ref, back_ref, out_ref):
    total = back_ref.shape[0] * back_ref.shape[1]
    count = at_ref.shape[1]
    pick = (lax.broadcasted_iota(jnp.int32, (total, count), 0) == at_ref[...]).astype(F32)
    back = back_ref[...].reshape(total, back_ref.shape[2])
    out_ref[...] = lax.dot_general(
        pick.astype(BF), back, (((0,), (0,)), ((), ())), preferred_element_type=F32
    ).astype(BF)


def ring_of(n_dp):
    if n_dp == 8:
        return [0, 2, 4, 6, 7, 5, 3, 1]
    order = []
    for block in range(n_dp // 4):
        line = list(range(block * 4, block * 4 + 4))
        order += line if block % 2 == 0 else line[::-1]
    return order


def on_device(patches, kept_mask, destination, coefficients, cotangent):
    n_dp = lax.axis_size("dp")
    n_mp = lax.axis_size("mp")
    img_dev, block_len, features = patches.shape
    channels, _, hidden = coefficients.shape
    capacity = img_dev * (KEEP_IMG // n_mp + KEEP_IMG // (2 * n_mp)) // n_dp
    slots = -(-(capacity + 1) // 8) * 8
    own = img_dev * (KEEP_IMG // n_mp)
    all_rows = own * n_mp
    patch_count = img_dev * block_len
    share = features // n_dp
    width = -(-own // 128) * 128

    ring = ring_of(n_dp)
    n_steps = n_dp // 2
    place = {device: index for index, device in enumerate(ring)}
    table = np.zeros((n_dp, n_mp, 4 + n_dp), np.int32)
    for device in range(n_dp):
        for part in range(n_mp):
            for k in range(4):
                table[device, part, k] = part ^ k
            for shift in range(n_dp):
                table[device, part, 4 + shift] = ring[(place[device] - shift) % n_dp]
    index = lax.axis_index("dp") * n_mp + lax.axis_index("mp")
    meta = lax.dynamic_index_in_dim(
        jnp.asarray(table.reshape(n_dp * n_mp, -1)), index, 0, keepdims=False
    )
    forth = [(ring[i], ring[(i + 1) % n_dp]) for i in range(n_dp)]
    back = [(b, a) for a, b in forth]
    swap_core = [(i, i ^ 1) for i in range(n_mp)]
    swap_far = [(i, i ^ 2) for i in range(n_mp)]

    def vm(shape, dtype):
        return jax.ShapeDtypeStruct(shape, dtype)

    outgoing, at = pl.pallas_call(
        functools.partial(send_kernel, n_dp, slots, capacity),
        out_shape=(vm((n_dp * slots, features), BF), vm((1, patch_count), jnp.int32)),
        compiler_params=PARAMS,
        cost_estimate=cost(2 * n_dp * slots * patch_count * features, 4 * 2**20),
        name="send",
    )(kept_mask, destination, patches.reshape(patch_count, features))
    arrived = lax.all_to_all(
        outgoing.reshape(n_dp, slots, features), "dp", split_axis=0, concat_axis=0
    )

    rounds = []
    right = left = cotangent
    for _ in range(n_steps - 1):
        right = lax.ppermute(right, "dp", forth)
        left = lax.ppermute(left, "dp", back)
        rounds.append((right, left))
    half = all_rows // 2
    rounds.append(
        (lax.ppermute(right[:half], "dp", forth), lax.ppermute(left[half:], "dp", back))
    )

    group = 3
    hidden_grads = []
    for first in range(0, channels, group):
        hidden_grads.append(
            pl.pallas_call(
                hidden_kernel,
                grid=(group,),
                in_specs=[
                    pl.BlockSpec((all_rows, hidden), lambda c: (0, 0)),
                    pl.BlockSpec((1, features, hidden), lambda c, first=first: (c + first, 0, 0)),
                ],
                out_specs=pl.BlockSpec((1, all_rows, features), lambda c: (c, 0, 0)),
                out_shape=vm((group, all_rows, features), BF),
                compiler_params=PARAMS,
                cost_estimate=cost(
                    2 * group * all_rows * features * hidden,
                    group * features * (hidden + all_rows) * 2,
                ),
                name="hidden",
            )(cotangent, coefficients)
        )

    normed, feats, centred, inv_scale, pick = pl.pallas_call(
        functools.partial(arrive_kernel, n_dp, slots, capacity, own),
        out_shape=(
            vm((own, features), BF),
            vm((n_dp, share // 2, 2 * own), BF),
            vm((own, features), F32),
            vm((own, 128), F32),
            vm((n_dp * slots, width), BF),
        ),
        scratch_shapes=[pltpu.VMEM((n_dp * slots, width), F32)],
        compiler_params=PARAMS,
        cost_estimate=cost(2 * n_dp * slots * width * features, 4 * 2**20),
        name="arrive",
    )(arrived)

    norm_core = lax.ppermute(normed, "mp", swap_core)
    norm_far = lax.ppermute(normed, "mp", swap_far)
    norm_diag = lax.ppermute(norm_far, "mp", swap_core)

    def slope(values, k, dtype):
        block = 256
        return pl.pallas_call(
            functools.partial(slope_kernel, len(hidden_grads)),
            grid_spec=pltpu.PrefetchScalarGridSpec(
                num_scalar_prefetch=1,
                grid=(features // block,),
                in_specs=[
                    pl.BlockSpec((group, own, block), lambda f, meta, k=k: (0, meta[k], f))
                    for _ in hidden_grads
                ]
                + [pl.BlockSpec((own, block), lambda f, meta: (0, f))],
                out_specs=pl.BlockSpec((own, block), lambda f, meta: (0, f)),
            ),
            out_shape=vm((own, features), dtype),
            compiler_params=PARAMS,
            cost_estimate=cost(4e9, channels * own * features * 2),
            name="slope",
        )(meta, *hidden_grads, values)

    part_core = slope(norm_core, 1, BF)
    part_own = slope(normed, 0, F32)
    part_diag = slope(norm_diag, 3, BF)
    part_far = slope(norm_far, 2, F32)
    got_own = lax.ppermute(part_core, "mp", swap_core)
    got_far = lax.ppermute(part_diag, "mp", swap_core)
    far_sum = (part_far + got_far.astype(F32)).astype(BF)
    got_sum = lax.ppermute(far_sum, "mp", swap_far)

    back_slots = pl.pallas_call(
        reduce_kernel,
        out_shape=vm((n_dp, slots, features), BF),
        compiler_params=PARAMS,
        cost_estimate=cost(2 * n_dp * slots * own * features, 4 * 2**20),
        name="reduce",
    )(part_own, got_own, got_sum, centred, inv_scale, pick)
    returned = lax.all_to_all(back_slots, "dp", split_axis=0, concat_axis=0)
    owner_rows = pl.pallas_call(
        place_kernel,
        out_shape=vm((patch_count, features), BF),
        compiler_params=PARAMS,
        cost_estimate=cost(2 * n_dp * slots * patch_count * features, 3 * 2**20),
        name="place",
    )(at, returned)

    feat_own = lax.all_to_all(feats, "dp", split_axis=0, concat_axis=0)
    feat_core = lax.ppermute(feat_own, "mp", swap_core)
    feat_far = lax.ppermute(feat_own, "mp", swap_far)
    feat_diag = lax.ppermute(feat_far, "mp", swap_core)
    merge_spec = pl.BlockSpec((1, share // 2, 2 * own), lambda s, meta: (s, 0, 0))
    values = pl.pallas_call(
        merge_kernel,
        grid_spec=pltpu.PrefetchScalarGridSpec(
            num_scalar_prefetch=1,
            grid=(n_dp,),
            in_specs=[merge_spec] * 4,
            out_specs=pl.BlockSpec((1, share, all_rows), lambda s, meta: (s, 0, 0)),
        ),
        out_shape=vm((n_dp, share, all_rows), BF),
        compiler_params=PARAMS,
        cost_estimate=cost(1e9, 4 * 2**20),
        name="merge",
    )(meta, feat_own, feat_core, feat_far, feat_diag)

    def table_sum(items, running):
        spans = [span for _, _, span in items]
        value_specs = [
            pl.BlockSpec((1, share, all_rows), lambda i, meta, shift=shift: (meta[4 + shift], 0, 0))
            for shift, _, _ in items
        ]
        cot_specs = [pl.BlockSpec(cot.shape, lambda i, meta: (0, 0)) for _, cot, _ in items]
        whole = pl.BlockSpec((channels, share, hidden), lambda i, meta: (0, 0, 0))
        extra = [] if running is None else [running]
        rows = sum(high - low for low, high in spans)
        return pl.pallas_call(
            functools.partial(table_kernel, spans, bool(extra)),
            grid_spec=pltpu.PrefetchScalarGridSpec(
                num_scalar_prefetch=1,
                grid=(1,),
                in_specs=value_specs + cot_specs + [whole] * len(extra),
                out_specs=whole,
                scratch_shapes=[pltpu.VMEM((channels, share, all_rows), BF)],
            ),
            out_shape=vm((channels, share, hidden), F32),
            compiler_params=PARAMS,
            cost_estimate=cost(4 * channels * share * hidden * rows, 8 * 2**20),
            name="table",
        )(meta, *([values] * len(items)), *[cot for _, cot, _ in items], *extra)

    running = None
    items = [(0, cotangent, (0, all_rows))]
    for step, (right, left) in enumerate(rounds, 1):
        if step < n_steps:
            items += [(step, right, (0, all_rows)), (n_dp - step, left, (0, all_rows))]
        else:
            items += [(step, right, (0, half)), (step, left, (half, all_rows))]
        running = table_sum(items, running)
        items = []

    return (owner_rows.reshape(img_dev, block_len, features), running)


def solution(mesh):
    in_specs = (
        P("dp", "mp", None),
        P("dp", "mp"),
        P("dp", "mp"),
        P(None, None, "mp"),
        P("dp", "mp"),
    )
    out_specs = (P("dp", "mp", None), P(None, "dp", "mp"))
    return jax.shard_map(
        on_device, mesh=mesh, in_specs=in_specs, out_specs=out_specs, check_vma=False
    )
```

time: 768 us -> 203 us (0.26)
  waiting for transfers between devices: 510 us -> 31.5 us
  other arithmetic: 128 us -> 1.28 us
  Pallas kernels: 0 us -> 119 us
  matrix products: 56.2 us -> 0 us
  local copies, waits for them, and re-layouts: 36.1 us -> 11.5 us
  starting transfers between devices: 19.5 us -> 37.4 us
  between operations: 14 us -> 0.78 us
    reduce_scatter x2 -> x0, waiting for transfers between devices: 426 us -> none  [the longest x1 426 us: on_device(): lax.psum_scatter(jnp.einsum('tkf,tj->fkj', expanded, cotangent, preferred...]
    pallas_call x0 -> x16, Pallas kernels: none -> 119 us  [the longest x4 45.5 us: table_sum(): pl.pallas_call(functools.partial(table_kernel, spans, bool(extra)), grid_...]
    dot_general x5 -> x0, matrix products: 56.2 us -> none  [the longest x4 33.4 us: one_piece(): lax.dot_general(cot_rows, coef_table, (((1,), (1,)), ((), ())), preferred...]
    all_to_all x3, waiting for transfers between devices: 63.1 us -> 20.1 us  [the longest x1 20.1 us: on_device(): lax.all_to_all(outgoing.reshape(n_dp, slots, features), 'dp', split_axis=...]
    another operation x4 -> x0, other arithmetic: 42.8 us -> none
    div x6 -> x0, other arithmetic: 40.3 us -> none  [the longest x4 40.3 us: expand_slope(): cardinal_slope(knot_offsets(values)) / STEP_WIDTH]
    all_gather x1 -> x0, waiting for transfers between devices: 20.6 us -> none  [on_device(): normed_all = lax.all_gather(normed, 'mp', axis=0, tiled=True)]
    reduce_sum x8 -> x0, other arithmetic: 19.3 us -> none  [the longest x4 17.2 us: one_piece(): return jnp.sum(hidden_grad * expand_slope(value_rows), axis=1)]
  transfers between devices with their start and end apart: 6 -> 20, of which waited for: 4 -> 3; matrix products, arithmetic and copies ran while one was open for 11% -> 2% of each run, Pallas kernels for 0% -> 55%
where the time goes in v1:
time: 203 us; the launch traced here: 201 us
  Pallas kernels  119 us (59%)
  starting transfers between devices  37.4 us (18%)
  waiting for transfers between devices  31.5 us (16%)
  local copies, waits for them, and re-layouts  11.5 us (6%)
    pallas_call x4, Pallas kernels, table_sum(): pl.pallas_call(functools.partial(table_kernel, spans, bool(extra)), grid_...  45.5 us
    pallas_call x4, Pallas kernels, slope(): pl.pallas_call(functools.partial(slope_kernel, len(hidden_grads)), grid_s...  26.6 us
    pallas_call x3, Pallas kernels, on_device(): pl.pallas_call(hidden_kernel, grid=(group,), in_specs=[pl.BlockSpec((all_...  26 us
    all_to_all x1, waiting for transfers between devices, on_device(): lax.all_to_all(outgoing.reshape(n_dp, slots, features), 'dp', split_axis=...  20.1 us
    ppermute x3, starting transfers between devices, on_device(): right = lax.ppermute(right, 'dp', forth)  8.25 us
    unnamed x32, local copies, waits for them, and re-layouts  8.09 us
    all_to_all x1, starting transfers between devices, on_device(): lax.all_to_all(outgoing.reshape(n_dp, slots, features), 'dp', split_axis=...  7.31 us
    pallas_call x1, Pallas kernels, on_device(): pl.pallas_call(merge_kernel, grid_spec=pltpu.PrefetchScalarGridSpec(num_s...  6.61 us
  transfers between devices with their start and end apart: 20, of which 3 were waited for; matrix products, arithmetic and copies ran while one was open for 2% of the time, Pallas kernels for 55%

profile of v1, /device:TPU:0, one launch (start us, length us, event | category | flops | bytes accessed | tf_op | source)
XLA Modules:
  0.0 201.4 jit_solution(6727329064912341055)
XLA Ops:
  0.6 3.6 %send.1 = (bf16[320,1280]{1,0:T(8,128)(2,1)}, s32[1,768]{1,0:T(1,128)}) custom-call(s32[3,256]{1,0:T(4,128)} %kept_ref.1, s32[3,256]{1,0:T(4,128)} %dest_ref.1, bf16[768,1280]{1,0:T(8,128)(2,1)} %bitcast.7), custom_call_target="tpu_custom_call" | custom-call | flops 629145600 | bytes 4194304 | tf_op jit(solution)/shard_map/send/pallas_call | solution.py:304
  4.2 7.3 %all-to-all-start = ((bf16[8,40,1280]{2,1,0:T(8,128)(2,1)}), bf16[8,40,1280]{2,1,0:T(8,128)(2,1)S(1)}, u32[]{:S(2)}, u32[]{:S(2)}) async-start(bf16[8,40,1280]{2,1,0:T(8,128)(2,1)} %bitcast.6), calls=%async_computation | async-start | bytes 1638400 | tf_op jit(solution)/shard_map/all_to_all | solution.py:311
  13.6 20.1 %all-to-all-done.in_ref = bf16[8,40,1280]{2,1,0:T(8,128)(2,1)S(1)} async-done(((bf16[8,40,1280]{2,1,0:T(8,128)(2,1)}), bf16[8,40,1280]{2,1,0:T(8,128)(2,1)S(1)}, u32[]{:S(2)}, u32[]{:S(2)}) %all-to-all-start) | async-done | bytes 819232 | tf_op jit(solution)/shard_map/all_to_all | solution.py:311
  34.6 3.4 %arrive.1 = (bf16[192,1280]{1,0:T(8,128)(2,1)}, bf16[8,80,384]{2,1,0:T(8,128)(2,1)}, f32[192,1280]{1,0:T(8,128)}, f32[192,128]{1,0:T(8,128)}, bf16[320,256]{1,0:T(8,128)(2,1)}) custom-call(bf16[8,40,1280]{2,1,0:T(8,128)(2,1)} %copy-done.2), custom_call_target="tpu_custom_call" | custom-call | flops 209715200 | bytes 4194304 | tf_op jit(solution)/shard_map/arrive/pallas_call | solution.py:348
  39.6 6.3 %collective-permute-done.9.refs_4_ = bf16[768,640]{1,0:T(8,128)(2,1)} collective-permute-done((bf16[768,640]{1,0:T(8,128)(2,1)S(1)}, bf16[768,640]{1,0:T(8,128)(2,1)}, u32[]{:S(2)}, u32[]{:S(2)}) %collective-permute-start.9) | collective-permute-done | bytes 983072 | tf_op jit(solution)/shard_map/ppermute | solution.py:318
  45.9 5.9 %collective-permute-start.10 = (bf16[768,640]{1,0:T(8,128)(2,1)}, bf16[768,640]{1,0:T(8,128)(2,1)}, u32[]{:S(2)}, u32[]{:S(2)}) collective-permute-start(bf16[768,640]{1,0:T(8,128)(2,1)} %collective-permute-done.9.refs_4_), channel_id=1, source_target_pairs={{0,8},{8,16},{16,24},{24,28},{28,20},{20,12},{12,4},{4,0},{1,9},{9... | collective-permute-start | bytes 2949128 | tf_op jit(solution)/shard_map/ppermute | solution.py:318
  51.8 5.9 %all-to-all-start.2 = ((bf16[8,80,384]{2,1,0:T(8,128)(2,1)}), bf16[8,80,384]{2,1,0:T(8,128)(2,1)S(1)}, u32[]{:S(2)}, u32[]{:S(2)}) async-start(bf16[8,80,384]{2,1,0:T(8,128)(2,1)} %get-tuple-element.15), calls=%async_computation.2 | async-start | bytes 983040 | tf_op jit(solution)/shard_map/all_to_all | solution.py:412
  57.7 8.6 %hidden.3.refs_0_ = bf16[3,768,1280]{2,1,0:T(8,128)(2,1)} custom-call(bf16[768,640]{1,0:T(8,128)(2,1)} %refs_3_.1, bf16[9,1280,640]{2,1,0:T(8,128)(2,1)} %coef_ref.5), custom_call_target="tpu_custom_call" | custom-call | flops 3774873600 | bytes 10813440 | tf_op jit(solution)/shard_map/hidden/pallas_call | solution.py:330
  66.4 8.8 %hidden.4.refs_1_ = bf16[3,768,1280]{2,1,0:T(8,128)(2,1)} custom-call(bf16[768,640]{1,0:T(8,128)(2,1)} %refs_3_.1, bf16[9,1280,640]{2,1,0:T(8,128)(2,1)} %coef_ref.5), custom_call_target="tpu_custom_call" | custom-call | flops 3774873600 | bytes 10813440 | tf_op jit(solution)/shard_map/hidden/pallas_call | solution.py:330
  75.2 2.1 %collective-permute-start.14 = (bf16[768,640]{1,0:T(8,128)(2,1)}, bf16[768,640]{1,0:T(8,128)(2,1)}, u32[]{:S(2)}, u32[]{:S(2)}) collective-permute-start(bf16[768,640]{1,0:T(8,128)(2,1)} %collective-permute-done.13.refs_5_), channel_id=1, source_target_pairs={{8,0},{16,8},{24,16},{28,24},{20,28},{12,20},{4,12},{0,4},{9,1},{1... | collective-permute-start | bytes 2949128 | tf_op jit(solution)/shard_map/ppermute | solution.py:319
  77.3 8.6 %hidden.5.refs_2_ = bf16[3,768,1280]{2,1,0:T(8,128)(2,1)} custom-call(bf16[768,640]{1,0:T(8,128)(2,1)} %refs_3_.1, bf16[9,1280,640]{2,1,0:T(8,128)(2,1)} %coef_ref.5), custom_call_target="tpu_custom_call" | custom-call | flops 3774873600 | bytes 10813440 | tf_op jit(solution)/shard_map/hidden/pallas_call | solution.py:330
  89.7 6.5 %slope.7 = bf16[192,1280]{1,0:T(8,128)(2,1)} custom-call(s32[12]{0:T(128)} %dynamic-slice_bitcast_fusion.meta_ref, bf16[3,768,1280]{2,1,0:T(8,128)(2,1)} %hidden.3.refs_0_, bf16[3,768,1280]{2,1,0:T(8,128)(2,1)} %hidden.4.refs_1_, bf16[3,768,1280]{2,1,0:T(8,128)(2,1)} %hidden.5.refs_2_, bf16[192,1280]{1,0:T(8,128)(2,1)} %copy-done.7), custom_call_target="tpu_custom_call" | custom-call | flops 4000000000 | bytes 4423680 | tf_op jit(solution)/shard_map/slope/pallas_call | solution.py:369
  97.0 6.5 %slope.5 = bf16[192,1280]{1,0:T(8,128)(2,1)} custom-call(s32[12]{0:T(128)} %dynamic-slice_bitcast_fusion.meta_ref, bf16[3,768,1280]{2,1,0:T(8,128)(2,1)} %hidden.3.refs_0_, bf16[3,768,1280]{2,1,0:T(8,128)(2,1)} %hidden.4.refs_1_, bf16[3,768,1280]{2,1,0:T(8,128)(2,1)} %hidden.5.refs_2_, bf16[192,1280]{1,0:T(8,128)(2,1)} %copy-done.8), custom_call_target="tpu_custom_call" | custom-call | flops 4000000000 | bytes 4423680 | tf_op jit(solution)/shard_map/slope/pallas_call | solution.py:369
  105.7 6.8 %slope.6 = f32[192,1280]{1,0:T(8,128)} custom-call(s32[12]{0:T(128)} %dynamic-slice_bitcast_fusion.meta_ref, bf16[3,768,1280]{2,1,0:T(8,128)(2,1)} %hidden.3.refs_0_, bf16[3,768,1280]{2,1,0:T(8,128)(2,1)} %hidden.4.refs_1_, bf16[3,768,1280]{2,1,0:T(8,128)(2,1)} %hidden.5.refs_2_, bf16[192,1280]{1,0:T(8,128)(2,1)} %copy-done.5), custom_call_target="tpu_custom_call" | custom-call | flops 4000000000 | bytes 4423680 | tf_op jit(solution)/shard_map/slope/pallas_call | solution.py:369
  115.0 6.9 %slope.4.own_ref = f32[192,1280]{1,0:T(8,128)} custom-call(s32[12]{0:T(128)} %dynamic-slice_bitcast_fusion.meta_ref, bf16[3,768,1280]{2,1,0:T(8,128)(2,1)} %hidden.3.refs_0_, bf16[3,768,1280]{2,1,0:T(8,128)(2,1)} %hidden.4.refs_1_, bf16[3,768,1280]{2,1,0:T(8,128)(2,1)} %hidden.5.refs_2_, bf16[192,1280]{1,0:T(8,128)(2,1)} %get-tuple-element.11.refs_3_), custom_call_target="tpu_custom_call" | custom-call | flops 4000000000 | bytes 4423680 | tf_op jit(solution)/shard_map/slope/pallas_call | solution.py:369
  122.9 5.0 %collective-permute-done.15.refs_3_ = bf16[768,640]{1,0:T(8,128)(2,1)S(1)} collective-permute-done((bf16[768,640]{1,0:T(8,128)(2,1)}, bf16[768,640]{1,0:T(8,128)(2,1)S(1)}, u32[]{:S(2)}, u32[]{:S(2)}) %collective-permute-start.15) | collective-permute-done | bytes 983072 | tf_op jit(solution)/shard_map/ppermute | solution.py:319
  133.3 6.6 %merge.1.refs_0_.refs_1_.refs_2_ = bf16[8,160,768]{2,1,0:T(8,128)(2,1)} custom-call(s32[12]{0:T(128)} %dynamic-slice_bitcast_fusion.meta_ref, bf16[8,80,384]{2,1,0:T(8,128)(2,1)} %copy-done.3, bf16[8,80,384]{2,1,0:T(8,128)(2,1)} %copy-done.11, bf16[8,80,384]{2,1,0:T(8,128)(2,1)} %copy-done.6, bf16[8,80,384]{2,1,0:T(8,128)(2,1)} %copy-done.12), custom_call_target="tpu_custom_call" | custom-call | flops 1000000000 | bytes 4194304 | tf_op jit(solution)/shard_map/merge/pallas_call | solution.py:417
  140.9 3.6 %reduce.1 = bf16[8,40,1280]{2,1,0:T(8,128)(2,1)} custom-call(f32[192,1280]{1,0:T(8,128)} %slope.4.own_ref, bf16[192,1280]{1,0:T(8,128)(2,1)} %copy-done.13, bf16[192,1280]{1,0:T(8,128)(2,1)} %copy-done.14, f32[192,1280]{1,0:T(8,128)} %get-tuple-element.12.wide_ref, f32[192,128]{1,0:T(8,128)} %get-tuple-element.13.inv_ref, ...), custom_call_target="tpu_custom_call" | custom-call | flops 157286400 | bytes 4194304 | tf_op jit(solution)/shard_map/reduce/pallas_call | solution.py:396
  144.4 5.3 %all-to-all-start.1 = ((bf16[8,40,1280]{2,1,0:T(8,128)(2,1)}), bf16[8,40,1280]{2,1,0:T(8,128)(2,1)S(1)}, u32[]{:S(2)}, u32[]{:S(2)}) async-start(bf16[8,40,1280]{2,1,0:T(8,128)(2,1)} %reduce.1), calls=%async_computation.1 | async-start | bytes 1638400 | tf_op jit(solution)/shard_map/all_to_all | solution.py:403
  149.8 13.6 %table.4.refs_4_ = f32[9,160,640]{2,1,0:T(8,128)} custom-call(s32[12]{0:T(128)} %dynamic-slice_bitcast_fusion.meta_ref, bf16[8,160,768]{2,1,0:T(8,128)(2,1)} %merge.1.refs_0_.refs_1_.refs_2_, bf16[8,160,768]{2,1,0:T(8,128)(2,1)} %merge.1.refs_0_.refs_1_.refs_2_, bf16[8,160,768]{2,1,0:T(8,128)(2,1)} %merge.1.refs_0_.refs_1_.refs_2_, ...), custom_call_target="tpu_custom_call" | custom-call | flops 8493465600 | bytes 8388608 | tf_op jit(solution)/shard_map/table/pallas_call | solution.py:441
  163.3 11.4 %table.5.refs_4_ = f32[9,160,640]{2,1,0:T(8,128)} custom-call(s32[12]{0:T(128)} %dynamic-slice_bitcast_fusion.meta_ref, bf16[8,160,768]{2,1,0:T(8,128)(2,1)} %merge.1.refs_0_.refs_1_.refs_2_, bf16[8,160,768]{2,1,0:T(8,128)(2,1)} %merge.1.refs_0_.refs_1_.refs_2_, bf16[768,640]{1,0:T(8,128)(2,1)} %collective-permute-done.10.refs_2_, ...), custom_call_target="tpu_custom_call" | custom-call | flops 5662310400 | bytes 8388608 | tf_op jit(solution)/shard_map/table/pallas_call | solution.py:441
  174.7 11.6 %table.6.refs_4_ = f32[9,160,640]{2,1,0:T(8,128)} custom-call(s32[12]{0:T(128)} %dynamic-slice_bitcast_fusion.meta_ref, bf16[8,160,768]{2,1,0:T(8,128)(2,1)} %merge.1.refs_0_.refs_1_.refs_2_, bf16[8,160,768]{2,1,0:T(8,128)(2,1)} %merge.1.refs_0_.refs_1_.refs_2_, bf16[768,640]{1,0:T(8,128)(2,1)} %collective-permute-done.11.refs_2_, ...), custom_call_target="tpu_custom_call" | custom-call | flops 5662310400 | bytes 8388608 | tf_op jit(solution)/shard_map/table/pallas_call | solution.py:441
  187.9 8.9 %table.7 = f32[9,160,640]{2,1,0:T(8,128)} custom-call(s32[12]{0:T(128)} %dynamic-slice_bitcast_fusion.meta_ref, bf16[8,160,768]{2,1,0:T(8,128)(2,1)} %merge.1.refs_0_.refs_1_.refs_2_, bf16[8,160,768]{2,1,0:T(8,128)(2,1)} %merge.1.refs_0_.refs_1_.refs_2_, bf16[384,640]{1,0:T(8,128)(2,1)} %copy-done.9, bf16[384,640]{1,0:T(8,128)(2,1)} %copy-done.10, ...), custom_call_target="tpu_custom_call" | custom-call | flops 2831155200 | bytes 8388608 | tf_op jit(solution)/shard_map/table/pallas_call | solution.py:441
  197.7 3.6 %place.1 = bf16[768,1280]{1,0:T(8,128)(2,1)} custom-call(s32[1,768]{1,0:T(1,128)} %get-tuple-element.9.at_ref, bf16[8,40,1280]{2,1,0:T(8,128)(2,1)} %copy-done.1), custom_call_target="tpu_custom_call" | custom-call | flops 629145600 | bytes 3145728 | tf_op jit(solution)/shard_map/place/pallas_call | solution.py:404
  (68 shorter events, 23.7 us)
Async XLA Ops:
  0.6 10.9 %copy-start = (bf16[768,640]{1,0:T(8,128)(2,1)S(1)}, bf16[768,640]{1,0:T(8,128)(2,1)}, u32[]{:S(2)}) copy-start(bf16[768,640]{1,0:T(8,128)(2,1)} %refs_3_.1) | copy-start | bytes 2949124
  4.2 29.5 %all-to-all-start = ((bf16[8,40,1280]{2,1,0:T(8,128)(2,1)}), bf16[8,40,1280]{2,1,0:T(8,128)(2,1)S(1)}, u32[]{:S(2)}, u32[]{:S(2)}) async-start(bf16[8,40,1280]{2,1,0:T(8,128)(2,1)} %bitcast.6), calls=%async_computation | async-start | bytes 1638400 | tf_op jit(solution)/shard_map/all_to_all | solution.py:311
  11.5 34.4 %collective-permute-start.9 = (bf16[768,640]{1,0:T(8,128)(2,1)S(1)}, bf16[768,640]{1,0:T(8,128)(2,1)}, u32[]{:S(2)}, u32[]{:S(2)}) collective-permute-start(bf16[768,640]{1,0:T(8,128)(2,1)S(1)} %copy-done), channel_id=1, source_target_pairs={{0,8},{8,16},{16,24},{24,28},{28,20},{20,12},{12,4},{4,0},{1,9},{9... | collective-permute-start | bytes 2949128 | tf_op jit(solution)/shard_map/ppermute | solution.py:318
  13.6 61.7 %collective-permute-start.13 = (bf16[768,640]{1,0:T(8,128)(2,1)S(1)}, bf16[768,640]{1,0:T(8,128)(2,1)}, u32[]{:S(2)}, u32[]{:S(2)}) collective-permute-start(bf16[768,640]{1,0:T(8,128)(2,1)S(1)} %copy-done), channel_id=1, source_target_pairs={{8,0},{16,8},{24,16},{28,24},{20,28},{12,20},{4,12},{0,4},{9,1},{1... | collective-permute-start | bytes 2949128 | tf_op jit(solution)/shard_map/ppermute | solution.py:319
  38.1 28.2 %collective-permute-start.2 = (bf16[192,1280]{1,0:T(8,128)(2,1)}, bf16[192,1280]{1,0:T(8,128)(2,1)S(1)}, u32[]{:S(2)}, u32[]{:S(2)}) collective-permute-start(bf16[192,1280]{1,0:T(8,128)(2,1)} %get-tuple-element.11.refs_3_), channel_id=1, source_target_pairs={{0,2},{1,3},{2,0},{3,1},{4,6},{5,7},{6,4},{7,5},{8,10},{9,11},{10,... | collective-permute-start | bytes 1474568 | tf_op jit(solution)/shard_map/ppermute | solution.py:364
  45.9 41.2 %collective-permute-start.10 = (bf16[768,640]{1,0:T(8,128)(2,1)}, bf16[768,640]{1,0:T(8,128)(2,1)}, u32[]{:S(2)}, u32[]{:S(2)}) collective-permute-start(bf16[768,640]{1,0:T(8,128)(2,1)} %collective-permute-done.9.refs_4_), channel_id=1, source_target_pairs={{0,8},{8,16},{16,24},{24,28},{28,20},{20,12},{12,4},{4,0},{1,9},{9... | collective-permute-start | bytes 2949128 | tf_op jit(solution)/shard_map/ppermute | solution.py:318
  51.8 35.6 %all-to-all-start.2 = ((bf16[8,80,384]{2,1,0:T(8,128)(2,1)}), bf16[8,80,384]{2,1,0:T(8,128)(2,1)S(1)}, u32[]{:S(2)}, u32[]{:S(2)}) async-start(bf16[8,80,384]{2,1,0:T(8,128)(2,1)} %get-tuple-element.15), calls=%async_computation.2 | async-start | bytes 983040 | tf_op jit(solution)/shard_map/all_to_all | solution.py:412
  66.3 11.0 %copy-start.4 = (bf16[192,1280]{1,0:T(8,128)(2,1)S(1)}, bf16[192,1280]{1,0:T(8,128)(2,1)}, u32[]{:S(2)}) copy-start(bf16[192,1280]{1,0:T(8,128)(2,1)} %get-tuple-element.11.refs_3_) | copy-start | bytes 1474564
  66.3 22.6 %collective-permute-start.3 = (bf16[192,1280]{1,0:T(8,128)(2,1)S(1)}, bf16[192,1280]{1,0:T(8,128)(2,1)S(1)}, u32[]{:S(2)}, u32[]{:S(2)}) collective-permute-start(bf16[192,1280]{1,0:T(8,128)(2,1)S(1)} %collective-permute-done.2.refs_3_), channel_id=1, source_target_pairs={{0,1},{1,0},{2,3},{3,2},{4,5},{5,4},{6,7},{7,6},{8,9},{9,8},{10,11... | collective-permute-start | bytes 1474568 | tf_op jit(solution)/shard_map/ppermute | solution.py:365
  75.2 28.8 %collective-permute-start.14 = (bf16[768,640]{1,0:T(8,128)(2,1)}, bf16[768,640]{1,0:T(8,128)(2,1)}, u32[]{:S(2)}, u32[]{:S(2)}) collective-permute-start(bf16[768,640]{1,0:T(8,128)(2,1)} %collective-permute-done.13.refs_5_), channel_id=1, source_target_pairs={{8,0},{16,8},{24,16},{28,24},{20,28},{12,20},{4,12},{0,4},{9,1},{1... | collective-permute-start | bytes 2949128 | tf_op jit(solution)/shard_map/ppermute | solution.py:319
  77.3 18.9 %collective-permute-start = (bf16[192,1280]{1,0:T(8,128)(2,1)S(1)}, bf16[192,1280]{1,0:T(8,128)(2,1)S(1)}, u32[]{:S(2)}, u32[]{:S(2)}) collective-permute-start(bf16[192,1280]{1,0:T(8,128)(2,1)S(1)} %copy-done.4), channel_id=1, source_target_pairs={{0,1},{1,0},{2,3},{3,2},{4,5},{5,4},{6,7},{7,6},{8,9},{9,8},{10,11... | collective-permute-start | bytes 1474568 | tf_op jit(solution)/shard_map/ppermute | solution.py:363
  87.1 27.2 %collective-permute-start.11 = (bf16[768,640]{1,0:T(8,128)(2,1)}, bf16[768,640]{1,0:T(8,128)(2,1)}, u32[]{:S(2)}, u32[]{:S(2)}) collective-permute-start(bf16[768,640]{1,0:T(8,128)(2,1)} %collective-permute-done.10.refs_2_), channel_id=1, source_target_pairs={{0,8},{8,16},{16,24},{24,28},{28,20},{20,12},{12,4},{4,0},{1,9},{9... | collective-permute-start | bytes 2949128 | tf_op jit(solution)/shard_map/ppermute | solution.py:318
  87.4 25.0 %copy-start.3 = (bf16[8,80,384]{2,1,0:T(8,128)(2,1)}, bf16[8,80,384]{2,1,0:T(8,128)(2,1)S(1)}, u32[]{:S(2)}) copy-start(bf16[8,80,384]{2,1,0:T(8,128)(2,1)S(1)} %all-to-all-done.2.own_ref) | copy-start | bytes 1474564
  87.5 25.0 %collective-permute-start.7 = (bf16[8,80,384]{2,1,0:T(8,128)(2,1)S(1)}, bf16[8,80,384]{2,1,0:T(8,128)(2,1)S(1)}, u32[]{:S(2)}, u32[]{:S(2)}) collective-permute-start(bf16[8,80,384]{2,1,0:T(8,128)(2,1)S(1)} %all-to-all-done.2.own_ref), channel_id=1, source_target_pairs={{0,2},{1,3},{2,0},{3,1},{4,6},{5,7},{6,4},{7,5},{8,10},{9,11},{10,... | collective-permute-start | bytes 1474568 | tf_op jit(solution)/shard_map/ppermute | solution.py:414
  96.2 16.3 %collective-permute-start.4 = (bf16[192,1280]{1,0:T(8,128)(2,1)}, bf16[192,1280]{1,0:T(8,128)(2,1)S(1)}, u32[]{:S(2)}, u32[]{:S(2)}) collective-permute-start(bf16[192,1280]{1,0:T(8,128)(2,1)} %slope.7), channel_id=1, source_target_pairs={{0,1},{1,0},{2,3},{3,2},{4,5},{5,4},{6,7},{7,6},{8,9},{9,8},{10,11... | collective-permute-start | bytes 1474568 | tf_op jit(solution)/shard_map/ppermute | solution.py:392
  103.5 36.4 %collective-permute-start.1 = (bf16[192,1280]{1,0:T(8,128)(2,1)}, bf16[192,1280]{1,0:T(8,128)(2,1)S(1)}, u32[]{:S(2)}, u32[]{:S(2)}) collective-permute-start(bf16[192,1280]{1,0:T(8,128)(2,1)} %slope.5), channel_id=1, source_target_pairs={{0,1},{1,0},{2,3},{3,2},{4,5},{5,4},{6,7},{7,6},{8,9},{9,8},{10,11... | collective-permute-start | bytes 1474568 | tf_op jit(solution)/shard_map/ppermute | solution.py:391
  104.0 23.9 %collective-permute-start.15 = (bf16[768,640]{1,0:T(8,128)(2,1)}, bf16[768,640]{1,0:T(8,128)(2,1)S(1)}, u32[]{:S(2)}, u32[]{:S(2)}) collective-permute-start(bf16[768,640]{1,0:T(8,128)(2,1)} %collective-permute-done.14.refs_3_), channel_id=1, source_target_pairs={{8,0},{16,8},{24,16},{28,24},{20,28},{12,20},{4,12},{0,4},{9,1},{1... | collective-permute-start | bytes 2949128 | tf_op jit(solution)/shard_map/ppermute | solution.py:319
  112.5 9.4 %copy-start.6 = (bf16[8,80,384]{2,1,0:T(8,128)(2,1)}, bf16[8,80,384]{2,1,0:T(8,128)(2,1)S(1)}, u32[]{:S(2)}) copy-start(bf16[8,80,384]{2,1,0:T(8,128)(2,1)S(1)} %collective-permute-done.7.far_ref) | copy-start | bytes 1474564
  112.5 19.3 %collective-permute-start.6 = (bf16[8,80,384]{2,1,0:T(8,128)(2,1)S(1)}, bf16[8,80,384]{2,1,0:T(8,128)(2,1)S(1)}, u32[]{:S(2)}, u32[]{:S(2)}) collective-permute-start(bf16[8,80,384]{2,1,0:T(8,128)(2,1)S(1)} %all-to-all-done.2.own_ref), channel_id=1, source_target_pairs={{0,1},{1,0},{2,3},{3,2},{4,5},{5,4},{6,7},{7,6},{8,9},{9,8},{10,11... | collective-permute-start | bytes 1474568 | tf_op jit(solution)/shard_map/ppermute | solution.py:413
  112.5 19.6 %collective-permute-start.8 = (bf16[8,80,384]{2,1,0:T(8,128)(2,1)S(1)}, bf16[8,80,384]{2,1,0:T(8,128)(2,1)S(1)}, u32[]{:S(2)}, u32[]{:S(2)}) collective-permute-start(bf16[8,80,384]{2,1,0:T(8,128)(2,1)S(1)} %collective-permute-done.7.far_ref), channel_id=1, source_target_pairs={{0,1},{1,0},{2,3},{3,2},{4,5},{5,4},{6,7},{7,6},{8,9},{9,8},{10,11... | collective-permute-start | bytes 1474568 | tf_op jit(solution)/shard_map/ppermute | solution.py:415
  114.3 25.6 %collective-permute-start.5 = (bf16[192,1280]{1,0:T(8,128)(2,1)S(1)}, bf16[192,1280]{1,0:T(8,128)(2,1)S(1)}, u32[]{:S(2)}, u32[]{:S(2)}) collective-permute-start(bf16[192,1280]{1,0:T(8,128)(2,1)S(1)} %add_convert_fusion), channel_id=1, source_target_pairs={{0,2},{1,3},{2,0},{3,1},{4,6},{5,7},{6,4},{7,5},{8,10},{9,11},{10,... | collective-permute-start | bytes 1474568 | tf_op jit(solution)/shard_map/ppermute | solution.py:394
  129.0 57.4 %collective-permute-start.12 = (bf16[384,640]{1,0:T(8,128)(2,1)S(1)}, bf16[384,640]{1,0:T(8,128)(2,1)S(1)}, u32[]{:S(2)}, u32[]{:S(2)}) collective-permute-start(bf16[384,640]{1,0:T(8,128)(2,1)S(1)} %slice.8), channel_id=1, source_target_pairs={{0,8},{8,16},{16,24},{24,28},{28,20},{20,12},{12,4},{4,0},{1,9},{9... | collective-permute-start | bytes 1474568 | tf_op jit(solution)/shard_map/ppermute | solution.py:323
  131.7 54.6 %collective-permute-start.16 = (bf16[384,640]{1,0:T(8,128)(2,1)S(1)}, bf16[384,640]{1,0:T(8,128)(2,1)S(1)}, u32[]{:S(2)}, u32[]{:S(2)}) collective-permute-start(bf16[384,640]{1,0:T(8,128)(2,1)S(1)} %slice.9), channel_id=1, source_target_pairs={{8,0},{16,8},{24,16},{28,24},{20,28},{12,20},{4,12},{0,4},{9,1},{1... | collective-permute-start | bytes 1474568 | tf_op jit(solution)/shard_map/ppermute | solution.py:323
  144.4 52.4 %all-to-all-start.1 = ((bf16[8,40,1280]{2,1,0:T(8,128)(2,1)}), bf16[8,40,1280]{2,1,0:T(8,128)(2,1)S(1)}, u32[]{:S(2)}, u32[]{:S(2)}) async-start(bf16[8,40,1280]{2,1,0:T(8,128)(2,1)} %reduce.1), calls=%async_computation.1 | async-start | bytes 1638400 | tf_op jit(solution)/shard_map/all_to_all | solution.py:403
  (12 other events, 18.2 us)
